TPU v7x, 256 devices: a whole 4x4x8 slice. The times are simulated.
256 devices in a mesh: row: 32 (over z, y), col: 8 (over x, core).
Axes of the slice: x: 4, y: 4, z: 8, core: 2. Of those that a mesh axis runs over, the one named last changes fastest.
Arguments:
- covariance: float32 [16384, 16384], P('row', 'col'), as said below
- courant: float32 [2, 16384], replicated, may hold values from 0.05 to 0.45
- upwind: int32 [16384], replicated, may hold values from 0 to 3
- observed: int32 [2, 256], replicated, may hold values from 0 to 16383
- noise: float32 [2, 256], replicated, may hold values from 0.5 to 2
Outputs:
- posterior: float32 [16384, 16384], P('row', 'col')
Inputs may be any that keep to these rules, and one draw needn't show every extreme that they name: The covariance is symmetric and positive definite.
All inputs are finite; a program needn't handle non-finite values.
Results may differ from a plain program's by a relative error of at most 0.0003.
Values sent between devices are 32-bit elements; how exact they have to be, the bound alone decides.
No kernel may reach another device: no remote copies, remote signals or barrier semaphores. Data moves between devices by JAX's collectives and lax.ppermute only.
A program may use at most 64 MiB of HBM per device.

v0:
```python
import jax
import jax.numpy as jnp
from jax import lax
from jax.sharding import PartitionSpec as P

G = 128
BATCHES = 2


def extended(block, sides, width):
    for axis, dim in sides:
        count = lax.axis_size(axis)
        forward = [(i, i + 1) for i in range(count - 1)]
        backward = [(target, source) for source, target in forward]
        low = lax.ppermute(
            lax.slice_in_dim(block, block.shape[dim] - width, None, axis=dim), axis, forward
        )
        high = lax.ppermute(lax.slice_in_dim(block, 0, width, axis=dim), axis, backward)
        block = jnp.concatenate([low, block, high], axis=dim)
    return block


def left_apply(padded, cour_a, cour_b, up_dir):
    lines = padded.shape[0] - 2
    center = padded[1:-1]
    prev_line = padded[:-2]
    next_line = padded[2:]
    prev_cell = jnp.pad(center, ((0, 0), (1, 0), (0, 0)))[:, :-1]
    next_cell = jnp.pad(center, ((0, 0), (0, 1), (0, 0)))[:, 1:]
    coef_a = cour_a.reshape(lines, G, 1)
    coef_b = cour_b.reshape(lines, G, 1)
    dirs = up_dir.reshape(lines, G, 1)
    up_line = jnp.where(dirs % 2 == 1, next_line, prev_line)
    up_cell = jnp.where(dirs // 2 == 1, next_cell, prev_cell)
    return (1.0 - coef_a - coef_b) * center + coef_a * up_line + coef_b * up_cell


def right_apply(padded, cour_a, cour_b, up_dir):
    lines = padded.shape[1] - 2
    center = padded[:, 1:-1]
    prev_line = padded[:, :-2]
    next_line = padded[:, 2:]
    prev_cell = jnp.pad(center, ((0, 0), (0, 0), (1, 0)))[:, :, :-1]
    next_cell = jnp.pad(center, ((0, 0), (0, 0), (0, 1)))[:, :, 1:]
    coef_a = cour_a.reshape(1, lines, G)
    coef_b = cour_b.reshape(1, lines, G)
    dirs = up_dir.reshape(1, lines, G)
    up_line = jnp.where(dirs % 2 == 1, next_line, prev_line)
    up_cell = jnp.where(dirs // 2 == 1, next_cell, prev_cell)
    return (1.0 - coef_a - coef_b) * center + coef_a * up_line + coef_b * up_cell


def transport(block, row_cour, row_dirs, col_cour, col_dirs):
    row_count, col_count = block.shape
    padded = extended(block, (("row", 0),), G)
    padded = padded.reshape(row_count // G + 2, G, col_count)
    block = left_apply(padded, row_cour[0], row_cour[1], row_dirs).reshape(row_count, col_count)
    padded = extended(block, (("col", 1),), G)
    padded = padded.reshape(row_count, col_count // G + 2, G)
    return right_apply(padded, col_cour[0], col_cour[1], col_dirs).reshape(row_count, col_count)


def shards(covariance, courant, upwind, observed, noise):
    row_count, col_count = covariance.shape
    row_start = lax.axis_index("row") * row_count
    col_start = lax.axis_index("col") * col_count
    row_cour = lax.dynamic_slice_in_dim(courant, row_start, row_count, 1)
    col_cour = lax.dynamic_slice_in_dim(courant, col_start, col_count, 1)
    row_dirs = lax.dynamic_slice_in_dim(upwind, row_start, row_count, 0)
    col_dirs = lax.dynamic_slice_in_dim(upwind, col_start, col_count, 0)
    block = covariance
    for cycle in range(BATCHES):
        block = transport(block, row_cour, row_dirs, col_cour, col_dirs)
        obs = observed[cycle]
        local_rows = obs - row_start
        owns_row = (local_rows >= 0) & (local_rows < row_count)
        row_pick = jnp.clip(local_rows, 0, row_count - 1)
        local_cols = obs - col_start
        owns_col = (local_cols >= 0) & (local_cols < col_count)
        col_pick = jnp.clip(local_cols, 0, col_count - 1)
        row_part = jnp.where(owns_row[:, None], jnp.take(block, row_pick, axis=0), 0.0)
        col_part = jnp.where(owns_col[None, :], jnp.take(block, col_pick, axis=1), 0.0)
        row_panel = lax.psum(row_part, "row")
        block_part = jnp.where(owns_col[None, :], jnp.take(row_panel, col_pick, axis=1), 0.0)
        col_panel, innov = lax.psum((col_part, block_part), "col")
        innov = innov + jnp.diag(noise[cycle])
        factor = jnp.linalg.cholesky(innov)
        gain = jax.scipy.linalg.cho_solve((factor, True), col_panel.T).T
        block = block - jnp.dot(
            gain, row_panel, precision=lax.Precision.HIGHEST, preferred_element_type=jnp.float32
        )
    return block


def solution(mesh):
    in_specs = (P("row", "col"), P(), P(), P(), P())
    out_specs = P("row", "col")
    return jax.shard_map(shards, mesh=mesh, in_specs=in_specs, out_specs=out_specs, check_vma=False)
```

profile of v0, /device:TPU:8, one launch (start us, length us, event | category | flops | bytes accessed | tf_op | source)
XLA Modules:
  0.0 755.2 jit_solution(8258046197964841338)
XLA Ops:
  9.2 4.1 collective-permute-start
  19.3 17.0 %collective-permute-done = f32[128,2048]{1,0:T(8,128)S(1)} collective-permute-done((f32[128,2048]{1,0:T(8,128)}, f32[128,2048]{1,0:T(8,128)S(1)}, u32[]{:S(2)}, u32[]{:S(2)}) %collective-permute-start) | collective-permute-done | bytes 1048608 | tf_op jit(solution)/shard_map/ppermute | solution.py:18
  38.1 3.8 pad_maximum_fusion.4
  45.2 5.3 copy.22
  54.2 4.0 collective-permute-done.3
  61.4 3.7 fusion.5
  65.1 5.4 copy.23
  70.5 4.6 gather_fusion
  76.9 3.4 gather_fusion.2
  81.2 158.6 %all-reduce.16.cloned.1.call-done = f32[256,2048]{1,0:T(8,128)} async-done(((f32[256,2048]{1,0:T(8,128)}), f32[256,2048]{1,0:T(8,128)}) %all-reduce.16.cloned.1.call-update) | async-done | bytes 2097168 | tf_op jit(solution)/shard_map/psum | solution.py:83
  243.9 65.5 %all-reduce.22.cloned.1.call-done = (f32[256,512]{1,0:T(8,128)}, f32[256,256]{0,1:T(8,128)}) async-done(((f32[256,512]{1,0:T(8,128)}, f32[256,256]{0,1:T(8,128)}), (f32[256,512]{1,0:T(8,128)}, f32[256,256]{0,1:T(8,128)})) %all-reduce.22.cloned.1.call-update) | async-done | bytes 786448 | tf_op jit(solution)/shard_map/psum | solution.py:85
  311.7 11.7 %cholesky.130 = f32[128,128]{1,0:T(8,128)S(1)} custom-call(f32[128,128]{1,0:T(8,128)S(1)} %cholesky.194), custom_call_target="Cholesky" | custom-call | tf_op jit(solution)/shard_map/jit(cholesky)/cholesky | solution.py:87
  323.5 9.8 %custom-call.15 = f32[1,128,128]{1,2,0:T(8,128)S(1)} custom-call(f32[1,128,128]{2,1,0:T(8,128)S(1)} %get-tuple-element.79), custom_call_target="InvertDiagBlocksLowerTriangular" | custom-call | tf_op jit(solution)/shard_map/jit(cholesky)/cholesky | solution.py:87
  333.8 11.7 %cholesky.147 = f32[128,128]{1,0:T(8,128)S(1)} custom-call(f32[128,128]{1,0:T(8,128)S(1)} %convolution_subtract_fusion.7), custom_call_target="Cholesky" | custom-call | tf_op jit(solution)/shard_map/jit(cholesky)/cholesky | solution.py:87
  348.2 4.1 while.4
  352.4 19.7 %custom-call.16 = f32[2,128,128]{1,2,0:T(8,128)S(1)} custom-call(f32[2,128,128]{2,1,0:T(8,128)S(1)} %get-tuple-element.24), custom_call_target="InvertDiagBlocksLowerTriangular" | custom-call | tf_op jit(solution)/shard_map/jit(_cho_solve)/triangular_solve | solution.py:88
  374.5 5.3 convolution_subtract_fusion.1
  382.5 3.4 collective-permute-start.5
  385.9 18.9 %collective-permute-done.4 = f32[128,2048]{1,0:T(8,128)S(1)} collective-permute-done((f32[128,2048]{1,0:T(8,128)S(1)}, f32[128,2048]{1,0:T(8,128)S(1)}, u32[]{:S(2)}, u32[]{:S(2)}) %collective-permute-start.4) | collective-permute-done | bytes 1048608 | tf_op jit(solution)/shard_map/ppermute | solution.py:18
  413.0 5.3 copy.24
  427.4 3.7 fusion.11
  431.1 5.4 copy.25
  436.5 4.6 gather_fusion.3
  442.8 3.4 gather_fusion.5
  447.2 159.6 %all-reduce.18.cloned.1.call-done = f32[256,2048]{1,0:T(8,128)} async-done(((f32[256,2048]{1,0:T(8,128)}), f32[256,2048]{1,0:T(8,128)}) %all-reduce.18.cloned.1.call-update) | async-done | bytes 2097168 | tf_op jit(solution)/shard_map/psum | solution.py:83
  611.0 65.8 %all-reduce.20.cloned.1.call-done = (f32[256,512]{1,0:T(8,128)}, f32[256,256]{0,1:T(8,128)}) async-done(((f32[256,512]{1,0:T(8,128)}, f32[256,256]{0,1:T(8,128)}), (f32[256,512]{1,0:T(8,128)}, f32[256,256]{0,1:T(8,128)})) %all-reduce.20.cloned.1.call-update) | async-done | bytes 786448 | tf_op jit(solution)/shard_map/psum | solution.py:85
  679.1 11.7 %cholesky.164 = f32[128,128]{1,0:T(8,128)S(1)} custom-call(f32[128,128]{1,0:T(8,128)S(1)} %cholesky.197), custom_call_target="Cholesky" | custom-call | tf_op jit(solution)/shard_map/jit(cholesky)/cholesky | solution.py:87
  690.9 9.8 %custom-call.17 = f32[1,128,128]{1,2,0:T(8,128)S(1)} custom-call(f32[1,128,128]{2,1,0:T(8,128)S(1)} %get-tuple-element.75), custom_call_target="InvertDiagBlocksLowerTriangular" | custom-call | tf_op jit(solution)/shard_map/jit(cholesky)/cholesky | solution.py:87
  701.2 11.7 %cholesky.181 = f32[128,128]{1,0:T(8,128)S(1)} custom-call(f32[128,128]{1,0:T(8,128)S(1)} %convolution_subtract_fusion.6), custom_call_target="Cholesky" | custom-call | tf_op jit(solution)/shard_map/jit(cholesky)/cholesky | solution.py:87
  715.5 3.9 while.5
  719.5 19.8 %custom-call.18 = f32[2,128,128]{1,2,0:T(8,128)S(1)} custom-call(f32[2,128,128]{2,1,0:T(8,128)S(1)} %get-tuple-element.25), custom_call_target="InvertDiagBlocksLowerTriangular" | custom-call | tf_op jit(solution)/shard_map/jit(_cho_solve)/triangular_solve | solution.py:88
  741.8 6.7 convolution_subtract_fusion
  (126 shorter events, 74.8 us)
Async XLA Ops:
  6.5 8.7 %copy-start.5 = (s32[2,256]{1,0:T(2,128)S(1)}, s32[2,256]{1,0:T(2,128)}, u32[]{:S(2)}) copy-start(s32[2,256]{1,0:T(2,128)} %param.17) | copy-start | bytes 6148
  6.5 233.3 %all-reduce.16.cloned.1.call-start = ((), (), s32[]{:S(2)}) async-start(), calls=%async_computation | async-start | bytes 4194304 | tf_op jit(solution)/shard_map/psum | solution.py:83
  9.2 27.0 %collective-permute-start = (f32[128,2048]{1,0:T(8,128)}, f32[128,2048]{1,0:T(8,128)S(1)}, u32[]{:S(2)}, u32[]{:S(2)}) collective-permute-start(f32[128,2048]{1,0:T(8,128)} %get-tuple-element.67), channel_id=1, source_target_pairs={{8,0},{16,8},{24,16},{32,24},{40,32},{48,40},{56,48},{64,56},{72,6... | collective-permute-start | bytes 3145736 | tf_op jit(solution)/shard_map/ppermute | solution.py:18
  13.3 24.8 %collective-permute-start.1 = (f32[128,2048]{1,0:T(8,128)S(1)}, f32[128,2048]{1,0:T(8,128)}, u32[]{:S(2)}, u32[]{:S(2)}) collective-permute-start(f32[128,2048]{1,0:T(8,128)S(1)} %get-tuple-element.66), channel_id=1, source_target_pairs={{0,8},{8,16},{16,24},{24,32},{32,40},{40,48},{48,56},{56,64},{64,7... | collective-permute-start | bytes 3145736 | tf_op jit(solution)/shard_map/ppermute | solution.py:15
  19.3 22.6 %copy-start = (f32[512,2048]{1,0:T(8,128)S(1)}, f32[512,2048]{1,0:T(8,128)}, u32[]{:S(2)}) copy-start(f32[512,2048]{1,0:T(8,128)} %param.14) | copy-start | bytes 12582916
  51.6 2.6 collective-permute-start.2
  52.9 5.3 collective-permute-start.3
  76.8 232.6 %all-reduce.22.cloned.1.call-start = ((), (), s32[]{:S(2)}) async-start(), calls=%async_computation.3 | async-start | bytes 1572864 | tf_op jit(solution)/shard_map/psum | solution.py:85
  81.2 162.7 %copy-start.6 = (f32[2,256]{1,0:T(2,128)S(1)}, f32[2,256]{1,0:T(2,128)}, u32[]{:S(2)}) copy-start(f32[2,256]{1,0:T(2,128)} %param.18) | copy-start | bytes 6148
  243.6 363.2 %all-reduce.18.cloned.1.call-start = ((), (), s32[]{:S(2)}) async-start(), calls=%async_computation.1 | async-start | bytes 4194304 | tf_op jit(solution)/shard_map/psum | solution.py:83
  309.4 62.7 %copy-start.3 = (f32[256,512]{1,0:T(8,128)S(1)}, f32[256,512]{1,0:T(8,128)}, u32[]{:S(2)}) copy-start(f32[256,512]{1,0:T(8,128)} %get-tuple-element.48) | copy-start | bytes 1572868
  310.4 64.0 %copy-start.1 = (f32[256,2048]{1,0:T(8,128)S(1)}, f32[256,2048]{1,0:T(8,128)}, u32[]{:S(2)}) copy-start(f32[256,2048]{1,0:T(8,128)} %all-reduce.16.cloned.1.call-done) | copy-start | bytes 6291460
  380.0 24.8 %collective-permute-start.4 = (f32[128,2048]{1,0:T(8,128)S(1)}, f32[128,2048]{1,0:T(8,128)S(1)}, u32[]{:S(2)}, u32[]{:S(2)}) collective-permute-start(f32[128,2048]{1,0:T(8,128)S(1)} %get-tuple-element.61), channel_id=1, source_target_pairs={{8,0},{16,8},{24,16},{32,24},{40,32},{48,40},{56,48},{64,56},{72,6... | collective-permute-start | bytes 3145736 | tf_op jit(solution)/shard_map/ppermute | solution.py:18
  382.5 24.6 %collective-permute-start.5 = (f32[128,2048]{1,0:T(8,128)S(1)}, f32[128,2048]{1,0:T(8,128)}, u32[]{:S(2)}, u32[]{:S(2)}) collective-permute-start(f32[128,2048]{1,0:T(8,128)S(1)} %get-tuple-element.60), channel_id=1, source_target_pairs={{0,8},{8,16},{16,24},{24,32},{32,40},{40,48},{48,56},{56,64},{64,7... | collective-permute-start | bytes 3145736 | tf_op jit(solution)/shard_map/ppermute | solution.py:15
  419.5 2.6 collective-permute-start.6
  420.8 3.4 collective-permute-start.7
  442.8 234.0 %all-reduce.20.cloned.1.call-start = ((), (), s32[]{:S(2)}) async-start(), calls=%async_computation.2 | async-start | bytes 1572864 | tf_op jit(solution)/shard_map/psum | solution.py:85
  676.8 62.5 %copy-start.4 = (f32[256,512]{1,0:T(8,128)S(1)}, f32[256,512]{1,0:T(8,128)}, u32[]{:S(2)}) copy-start(f32[256,512]{1,0:T(8,128)} %get-tuple-element.46) | copy-start | bytes 1572868
  677.8 63.9 %copy-start.2 = (f32[256,2048]{1,0:T(8,128)S(1)}, f32[256,2048]{1,0:T(8,128)}, u32[]{:S(2)}) copy-start(f32[256,2048]{1,0:T(8,128)} %all-reduce.18.cloned.1.call-done) | copy-start | bytes 6291460
Sparse Core Ops, SparseCore 0:
  76.9 162.9 all-reduce.15
  243.7 65.6 all-reduce.21
  442.9 163.9 all-reduce.17
  611.1 65.6 all-reduce.19
where the time goes:
time: 763 us; the launch traced here: 755 us
  waiting for transfers between devices  496 us (65%)
  other arithmetic  148 us (19%)
  local copies, waits for them, and re-layouts  59.5 us (8%)
  matrix products  17.7 us (2%)
  starting transfers between devices  17.3 us (2%)
  between operations  16.5 us (2%)
    psum x2, waiting for transfers between devices, shards(): row_panel = lax.psum(row_part, 'row')  318 us
    psum x2, waiting for transfers between devices, shards(): col_panel, innov = lax.psum((col_part, block_part), 'col')  131 us
    another operation x14, other arithmetic, shards(): factor = jnp.linalg.cholesky(innov)  69.2 us
    ppermute x4, waiting for transfers between devices, extended(): lax.ppermute(lax.slice_in_dim(block, 0, width, axis=dim), axis, backward)  41.9 us
    another operation x5, other arithmetic, shards(): gain = jax.scipy.linalg.cho_solve((factor, True), col_panel.T).T  39.6 us
  transfers between devices with their start and end apart: 12, of which 10 were waited for; matrix products, arithmetic and copies ran while one was open for 2% of the time, Pallas kernels for 0%

commit v1 on v0

--- a/solution.py
+++ b/solution.py
@@ -1,10 +1,23 @@
+import functools
 import jax
 import jax.numpy as jnp
 from jax import lax
 from jax.sharding import PartitionSpec as P
+from jax.lax import axis_size, ppermute
 
 G = 128
 BATCHES = 2
+
+
+def plane_draft(inp, mesh_dim):
+    num = axis_size(mesh_dim)
+    near = inp
+    for i0 in [[(ii, ii ^ at) for ii in range(num)] for at in (1, 2, 4, 8, 16) if at < num]:
+        near = near + ppermute(near, mesh_dim, perm=i0)
+    return near
+
+
+prepare_the_edge = functools.partial(plane_draft, mesh_dim="row")
 
 
 def extended(block, sides, width):
@@ -80,7 +93,7 @@
         col_pick = jnp.clip(local_cols, 0, col_count - 1)
         row_part = jnp.where(owns_row[:, None], jnp.take(block, row_pick, axis=0), 0.0)
         col_part = jnp.where(owns_col[None, :], jnp.take(block, col_pick, axis=1), 0.0)
-        row_panel = lax.psum(row_part, "row")
+        row_panel = prepare_the_edge(row_part)
         block_part = jnp.where(owns_col[None, :], jnp.take(row_panel, col_pick, axis=1), 0.0)
         col_panel, innov = lax.psum((col_part, block_part), "col")
         innov = innov + jnp.diag(noise[cycle])

time: 763 us -> 1150 us (1.51)
  waiting for transfers between devices: 496 us -> 835 us
  starting transfers between devices: 17.3 us -> 55.9 us
    ppermute x0 -> x10, waiting for transfers between devices: none -> 617 us  [plane_draft(): near = near + ppermute(near, mesh_dim, perm=i0)]
    psum x2 -> x0, waiting for transfers between devices: 318 us -> none  [shards(): row_panel = lax.psum(row_part, 'row')]
    psum x2, waiting for transfers between devices: 131 us -> 172 us  [shards(): col_panel, innov = lax.psum((col_part, block_part), 'col')]
    ppermute x0 -> x10, starting transfers between devices: none -> 38.7 us  [plane_draft(): near = near + ppermute(near, mesh_dim, perm=i0)]
    ppermute x4, waiting for transfers between devices: 4.12 us -> 20.7 us  [extended(): lax.ppermute(lax.slice_in_dim(block, block.shape[dim] - width, None, axis...]
    ppermute x4, waiting for transfers between devices: 41.9 us -> 26.2 us  [extended(): lax.ppermute(lax.slice_in_dim(block, 0, width, axis=dim), axis, backward)]
  transfers between devices with their start and end apart: 12 -> 20, of which waited for: 10 -> 18; matrix products, arithmetic and copies ran while one was open for 2% -> 1% of each run, Pallas kernels for 0% -> 0%
where the time goes in v1:
time: 1150 us; the launch traced here: 1140 us
  waiting for transfers between devices  835 us (73%)
  other arithmetic  153 us (13%)
  local copies, waits for them, and re-layouts  62.6 us (5%)
  starting transfers between devices  55.9 us (5%)
  matrix products  17.7 us (2%)
  between operations  17.2 us (1%)
    ppermute x10, waiting for transfers between devices, plane_draft(): near = near + ppermute(near, mesh_dim, perm=i0)  617 us
    psum x2, waiting for transfers between devices, shards(): col_panel, innov = lax.psum((col_part, block_part), 'col')  172 us
    another operation x14, other arithmetic, shards(): factor = jnp.linalg.cholesky(innov)  69.3 us
    another operation x5, other arithmetic, shards(): gain = jax.scipy.linalg.cho_solve((factor, True), col_panel.T).T  39.7 us
    ppermute x10, starting transfers between devices, plane_draft(): near = near + ppermute(near, mesh_dim, perm=i0)  38.7 us
    ppermute x4, waiting for transfers between devices, extended(): lax.ppermute(lax.slice_in_dim(block, 0, width, axis=dim), axis, backward)  26.2 us
  transfers between devices with their start and end apart: 20, of which 18 were waited for; matrix products, arithmetic and copies ran while one was open for 1% of the time, Pallas kernels for 0%

profile of v1, /device:TPU:8, one launch (start us, length us, event | category | flops | bytes accessed | tf_op | source)
XLA Modules:
  0.0 1142.2 jit_solution(14769491890301104347)
XLA Ops:
  19.3 17.0 %collective-permute-done = f32[128,2048]{1,0:T(8,128)S(1)} collective-permute-done((f32[128,2048]{1,0:T(8,128)}, f32[128,2048]{1,0:T(8,128)S(1)}, u32[]{:S(2)}, u32[]{:S(2)}) %collective-permute-start) | collective-permute-done | bytes 1048608 | tf_op jit(solution)/shard_map/ppermute | solution.py:31
  45.2 5.4 copy.22
  65.1 5.4 copy.23
  75.4 44.7 %collective-permute-done.4 = f32[256,2048]{1,0:T(8,128)S(1)} collective-permute-done((f32[256,2048]{1,0:T(8,128)S(1)}, f32[256,2048]{1,0:T(8,128)S(1)}, u32[]{:S(2)}, u32[]{:S(2)}) %collective-permute-start.4) | collective-permute-done | bytes 2097184 | tf_op jit(solution)/shard_map/ppermute | solution.py:16
  124.0 41.5 %collective-permute-done.5 = f32[256,2048]{1,0:T(8,128)S(1)} collective-permute-done((f32[256,2048]{1,0:T(8,128)S(1)}, f32[256,2048]{1,0:T(8,128)S(1)}, u32[]{:S(2)}, u32[]{:S(2)}) %collective-permute-start.5) | collective-permute-done | bytes 2097184 | tf_op jit(solution)/shard_map/ppermute | solution.py:16
  165.8 5.7 collective-permute-start.6
  171.5 43.6 %collective-permute-done.6 = f32[256,2048]{1,0:T(8,128)S(1)} collective-permute-done((f32[256,2048]{1,0:T(8,128)S(1)}, f32[256,2048]{1,0:T(8,128)S(1)}, u32[]{:S(2)}, u32[]{:S(2)}) %collective-permute-start.6) | collective-permute-done | bytes 2097184 | tf_op jit(solution)/shard_map/ppermute | solution.py:16
  215.5 5.1 collective-permute-start.7
  220.5 90.2 %collective-permute-done.7 = f32[256,2048]{1,0:T(8,128)S(1)} collective-permute-done((f32[256,2048]{1,0:T(8,128)S(1)}, f32[256,2048]{1,0:T(8,128)S(1)}, u32[]{:S(2)}, u32[]{:S(2)}) %collective-permute-start.7) | collective-permute-done | bytes 2097184 | tf_op jit(solution)/shard_map/ppermute | solution.py:16
  311.0 5.7 collective-permute-start.8
  321.1 88.1 %collective-permute-done.8 = f32[256,2048]{1,0:T(8,128)} collective-permute-done((f32[256,2048]{1,0:T(8,128)S(1)}, f32[256,2048]{1,0:T(8,128)}, u32[]{:S(2)}, u32[]{:S(2)}) %collective-permute-start.8) | collective-permute-done | bytes 2097184 | tf_op jit(solution)/shard_map/ppermute | solution.py:16
  417.0 95.8 %all-reduce.16.cloned.1.call-done = (f32[256,512]{1,0:T(8,128)}, f32[256,256]{0,1:T(8,128)}) async-done(((f32[256,512]{1,0:T(8,128)}, f32[256,256]{0,1:T(8,128)}), (f32[256,512]{1,0:T(8,128)}, f32[256,256]{0,1:T(8,128)})) %all-reduce.16.cloned.1.call-update) | async-done | bytes 786448 | tf_op jit(solution)/shard_map/psum | solution.py:98
  515.0 11.7 %cholesky.130 = f32[128,128]{1,0:T(8,128)S(1)} custom-call(f32[128,128]{1,0:T(8,128)S(1)} %cholesky.194), custom_call_target="Cholesky" | custom-call | tf_op jit(solution)/shard_map/jit(cholesky)/cholesky | solution.py:100
  526.8 9.8 custom-call.15
  537.1 11.7 %cholesky.147 = f32[128,128]{1,0:T(8,128)S(1)} custom-call(f32[128,128]{1,0:T(8,128)S(1)} %convolution_subtract_fusion.7), custom_call_target="Cholesky" | custom-call | tf_op jit(solution)/shard_map/jit(cholesky)/cholesky | solution.py:100
  556.2 19.7 %custom-call.16 = f32[2,128,128]{1,2,0:T(8,128)S(1)} custom-call(f32[2,128,128]{2,1,0:T(8,128)S(1)} %get-tuple-element.24), custom_call_target="InvertDiagBlocksLowerTriangular" | custom-call | tf_op jit(solution)/shard_map/jit(_cho_solve)/triangular_solve | solution.py:101
  578.3 5.3 convolution_subtract_fusion.1
  589.8 18.9 %collective-permute-done.10 = f32[128,2048]{1,0:T(8,128)S(1)} collective-permute-done((f32[128,2048]{1,0:T(8,128)S(1)}, f32[128,2048]{1,0:T(8,128)S(1)}, u32[]{:S(2)}, u32[]{:S(2)}) %collective-permute-start.10) | collective-permute-done | bytes 1048608 | tf_op jit(solution)/shard_map/ppermute | solution.py:28
  617.6 5.4 copy.24
  635.9 5.4 copy.25
  646.8 44.7 %collective-permute-done.13 = f32[256,2048]{1,0:T(8,128)S(1)} collective-permute-done((f32[256,2048]{1,0:T(8,128)S(1)}, f32[256,2048]{1,0:T(8,128)S(1)}, u32[]{:S(2)}, u32[]{:S(2)}) %collective-permute-start.13) | collective-permute-done | bytes 2097184 | tf_op jit(solution)/shard_map/ppermute | solution.py:16
  696.2 42.7 %collective-permute-done.14 = f32[256,2048]{1,0:T(8,128)S(1)} collective-permute-done((f32[256,2048]{1,0:T(8,128)S(1)}, f32[256,2048]{1,0:T(8,128)S(1)}, u32[]{:S(2)}, u32[]{:S(2)}) %collective-permute-start.14) | collective-permute-done | bytes 2097184 | tf_op jit(solution)/shard_map/ppermute | solution.py:16
  740.9 44.3 %collective-permute-done.15 = f32[256,2048]{1,0:T(8,128)S(1)} collective-permute-done((f32[256,2048]{1,0:T(8,128)S(1)}, f32[256,2048]{1,0:T(8,128)S(1)}, u32[]{:S(2)}, u32[]{:S(2)}) %collective-permute-start.15) | collective-permute-done | bytes 2097184 | tf_op jit(solution)/shard_map/ppermute | solution.py:16
  789.8 89.6 %collective-permute-done.16 = f32[256,2048]{1,0:T(8,128)S(1)} collective-permute-done((f32[256,2048]{1,0:T(8,128)S(1)}, f32[256,2048]{1,0:T(8,128)S(1)}, u32[]{:S(2)}, u32[]{:S(2)}) %collective-permute-start.16) | collective-permute-done | bytes 2097184 | tf_op jit(solution)/shard_map/ppermute | solution.py:16
  879.7 7.8 collective-permute-start.17
  891.9 87.2 %collective-permute-done.17 = f32[256,2048]{1,0:T(8,128)} collective-permute-done((f32[256,2048]{1,0:T(8,128)S(1)}, f32[256,2048]{1,0:T(8,128)}, u32[]{:S(2)}, u32[]{:S(2)}) %collective-permute-start.17) | collective-permute-done | bytes 2097184 | tf_op jit(solution)/shard_map/ppermute | solution.py:16
  987.0 76.1 %all-reduce.14.cloned.1.call-done = (f32[256,512]{1,0:T(8,128)}, f32[256,256]{0,1:T(8,128)}) async-done(((f32[256,512]{1,0:T(8,128)}, f32[256,256]{0,1:T(8,128)}), (f32[256,512]{1,0:T(8,128)}, f32[256,256]{0,1:T(8,128)})) %all-reduce.14.cloned.1.call-update) | async-done | bytes 786448 | tf_op jit(solution)/shard_map/psum | solution.py:98
  1065.2 11.7 %cholesky.164 = f32[128,128]{1,0:T(8,128)S(1)} custom-call(f32[128,128]{1,0:T(8,128)S(1)} %cholesky.197), custom_call_target="Cholesky" | custom-call | tf_op jit(solution)/shard_map/jit(cholesky)/cholesky | solution.py:100
  1077.0 9.8 custom-call.17
  1087.3 11.7 %cholesky.181 = f32[128,128]{1,0:T(8,128)S(1)} custom-call(f32[128,128]{1,0:T(8,128)S(1)} %convolution_subtract_fusion.6), custom_call_target="Cholesky" | custom-call | tf_op jit(solution)/shard_map/jit(cholesky)/cholesky | solution.py:100
  1105.9 19.9 %custom-call.18 = f32[2,128,128]{1,2,0:T(8,128)S(1)} custom-call(f32[2,128,128]{2,1,0:T(8,128)S(1)} %get-tuple-element.25), custom_call_target="InvertDiagBlocksLowerTriangular" | custom-call | tf_op jit(solution)/shard_map/jit(_cho_solve)/triangular_solve | solution.py:101
  1128.3 6.7 convolution_subtract_fusion
  (149 shorter events, 145.1 us)
Async XLA Ops:
  6.5 8.7 copy-start.5
  6.5 506.3 %all-reduce.16.cloned.1.call-start = ((), (), s32[]{:S(2)}) async-start(), calls=%async_computation.1 | async-start | bytes 1572864 | tf_op jit(solution)/shard_map/psum | solution.py:98
  9.2 27.0 %collective-permute-start = (f32[128,2048]{1,0:T(8,128)}, f32[128,2048]{1,0:T(8,128)S(1)}, u32[]{:S(2)}, u32[]{:S(2)}) collective-permute-start(f32[128,2048]{1,0:T(8,128)} %get-tuple-element.67), channel_id=1, source_target_pairs={{8,0},{16,8},{24,16},{32,24},{40,32},{48,40},{56,48},{64,56},{72,6... | collective-permute-start | bytes 3145736 | tf_op jit(solution)/shard_map/ppermute | solution.py:31
  13.3 24.8 %collective-permute-start.1 = (f32[128,2048]{1,0:T(8,128)S(1)}, f32[128,2048]{1,0:T(8,128)}, u32[]{:S(2)}, u32[]{:S(2)}) collective-permute-start(f32[128,2048]{1,0:T(8,128)S(1)} %get-tuple-element.66), channel_id=1, source_target_pairs={{0,8},{8,16},{16,24},{24,32},{32,40},{40,48},{48,56},{56,64},{64,7... | collective-permute-start | bytes 3145736 | tf_op jit(solution)/shard_map/ppermute | solution.py:28
  19.3 22.6 %copy-start = (f32[512,2048]{1,0:T(8,128)S(1)}, f32[512,2048]{1,0:T(8,128)}, u32[]{:S(2)}) copy-start(f32[512,2048]{1,0:T(8,128)} %param.14) | copy-start | bytes 12582916
  51.6 2.6 collective-permute-start.2
  52.9 5.3 collective-permute-start.3
  75.3 44.8 %collective-permute-start.4 = (f32[256,2048]{1,0:T(8,128)S(1)}, f32[256,2048]{1,0:T(8,128)S(1)}, u32[]{:S(2)}, u32[]{:S(2)}) collective-permute-start(f32[256,2048]{1,0:T(8,128)S(1)} %select_select_fusion.1), channel_id=1, source_target_pairs={{0,8},{8,0},{16,24},{24,16},{32,40},{40,32},{48,56},{56,48},{64,72... | collective-permute-start | bytes 6291464 | tf_op jit(solution)/shard_map/ppermute | solution.py:16
  120.5 45.0 %collective-permute-start.5 = (f32[256,2048]{1,0:T(8,128)S(1)}, f32[256,2048]{1,0:T(8,128)S(1)}, u32[]{:S(2)}, u32[]{:S(2)}) collective-permute-start(f32[256,2048]{1,0:T(8,128)S(1)} %fusion.80), channel_id=1, source_target_pairs={{0,16},{8,24},{16,0},{24,8},{32,48},{40,56},{48,32},{56,40},{64,80... | collective-permute-start | bytes 6291464 | tf_op jit(solution)/shard_map/ppermute | solution.py:16
  165.8 49.3 %collective-permute-start.6 = (f32[256,2048]{1,0:T(8,128)S(1)}, f32[256,2048]{1,0:T(8,128)S(1)}, u32[]{:S(2)}, u32[]{:S(2)}) collective-permute-start(f32[256,2048]{1,0:T(8,128)S(1)} %add.177), channel_id=1, source_target_pairs={{0,32},{8,40},{16,48},{24,56},{32,0},{40,8},{48,16},{56,24},{64,96... | collective-permute-start | bytes 6291464 | tf_op jit(solution)/shard_map/ppermute | solution.py:16
  215.5 95.3 %collective-permute-start.7 = (f32[256,2048]{1,0:T(8,128)S(1)}, f32[256,2048]{1,0:T(8,128)S(1)}, u32[]{:S(2)}, u32[]{:S(2)}) collective-permute-start(f32[256,2048]{1,0:T(8,128)S(1)} %add.178), channel_id=1, source_target_pairs={{0,64},{8,72},{16,80},{24,88},{32,96},{40,104},{48,112},{56,120},{... | collective-permute-start | bytes 6291464 | tf_op jit(solution)/shard_map/ppermute | solution.py:16
  311.0 10.1 copy-start.2
  311.0 98.2 %collective-permute-start.8 = (f32[256,2048]{1,0:T(8,128)S(1)}, f32[256,2048]{1,0:T(8,128)}, u32[]{:S(2)}, u32[]{:S(2)}) collective-permute-start(f32[256,2048]{1,0:T(8,128)S(1)} %add.179), channel_id=1, source_target_pairs={{0,128},{8,136},{16,144},{24,152},{32,160},{40,168},{48,176},{56,1... | collective-permute-start | bytes 6291464 | tf_op jit(solution)/shard_map/ppermute | solution.py:16
  411.7 5.3 copy-start.6
  417.0 646.1 %all-reduce.14.cloned.1.call-start = ((), (), s32[]{:S(2)}) async-start(), calls=%async_computation | async-start | bytes 1572864 | tf_op jit(solution)/shard_map/psum | solution.py:98
  512.8 63.0 %copy-start.3 = (f32[256,512]{1,0:T(8,128)S(1)}, f32[256,512]{1,0:T(8,128)}, u32[]{:S(2)}) copy-start(f32[256,512]{1,0:T(8,128)} %get-tuple-element.48) | copy-start | bytes 1572868
  583.8 24.8 %collective-permute-start.10 = (f32[128,2048]{1,0:T(8,128)S(1)}, f32[128,2048]{1,0:T(8,128)S(1)}, u32[]{:S(2)}, u32[]{:S(2)}) collective-permute-start(f32[128,2048]{1,0:T(8,128)S(1)} %get-tuple-element.60), channel_id=1, source_target_pairs={{0,8},{8,16},{16,24},{24,32},{32,40},{40,48},{48,56},{56,64},{64,7... | collective-permute-start | bytes 3145736 | tf_op jit(solution)/shard_map/ppermute | solution.py:28
  587.2 24.6 %collective-permute-start.9 = (f32[128,2048]{1,0:T(8,128)S(1)}, f32[128,2048]{1,0:T(8,128)}, u32[]{:S(2)}, u32[]{:S(2)}) collective-permute-start(f32[128,2048]{1,0:T(8,128)S(1)} %get-tuple-element.61), channel_id=1, source_target_pairs={{8,0},{16,8},{24,16},{32,24},{40,32},{48,40},{56,48},{64,56},{72,6... | collective-permute-start | bytes 3145736 | tf_op jit(solution)/shard_map/ppermute | solution.py:31
  624.1 2.6 collective-permute-start.11
  625.4 3.4 collective-permute-start.12
  646.1 45.4 %collective-permute-start.13 = (f32[256,2048]{1,0:T(8,128)S(1)}, f32[256,2048]{1,0:T(8,128)S(1)}, u32[]{:S(2)}, u32[]{:S(2)}) collective-permute-start(f32[256,2048]{1,0:T(8,128)S(1)} %select_select_fusion), channel_id=1, source_target_pairs={{0,8},{8,0},{16,24},{24,16},{32,40},{40,32},{48,56},{56,48},{64,72... | collective-permute-start | bytes 6291464 | tf_op jit(solution)/shard_map/ppermute | solution.py:16
  691.9 47.0 %collective-permute-start.14 = (f32[256,2048]{1,0:T(8,128)S(1)}, f32[256,2048]{1,0:T(8,128)S(1)}, u32[]{:S(2)}, u32[]{:S(2)}) collective-permute-start(f32[256,2048]{1,0:T(8,128)S(1)} %fusion.79), channel_id=1, source_target_pairs={{0,16},{8,24},{16,0},{24,8},{32,48},{40,56},{48,32},{56,40},{64,80... | collective-permute-start | bytes 6291464 | tf_op jit(solution)/shard_map/ppermute | solution.py:16
  739.3 46.0 %collective-permute-start.15 = (f32[256,2048]{1,0:T(8,128)S(1)}, f32[256,2048]{1,0:T(8,128)S(1)}, u32[]{:S(2)}, u32[]{:S(2)}) collective-permute-start(f32[256,2048]{1,0:T(8,128)S(1)} %add.187), channel_id=1, source_target_pairs={{0,32},{8,40},{16,48},{24,56},{32,0},{40,8},{48,16},{56,24},{64,96... | collective-permute-start | bytes 6291464 | tf_op jit(solution)/shard_map/ppermute | solution.py:16
  785.6 93.8 %collective-permute-start.16 = (f32[256,2048]{1,0:T(8,128)S(1)}, f32[256,2048]{1,0:T(8,128)S(1)}, u32[]{:S(2)}, u32[]{:S(2)}) collective-permute-start(f32[256,2048]{1,0:T(8,128)S(1)} %add.188), channel_id=1, source_target_pairs={{0,64},{8,72},{16,80},{24,88},{32,96},{40,104},{48,112},{56,120},{... | collective-permute-start | bytes 6291464 | tf_op jit(solution)/shard_map/ppermute | solution.py:16
  879.7 12.2 %copy-start.1 = (f32[256,2048]{1,0:T(8,128)}, f32[256,2048]{1,0:T(8,128)S(1)}, u32[]{:S(2)}) copy-start(f32[256,2048]{1,0:T(8,128)S(1)} %add.189) | copy-start | bytes 6291460
  879.7 99.3 %collective-permute-start.17 = (f32[256,2048]{1,0:T(8,128)S(1)}, f32[256,2048]{1,0:T(8,128)}, u32[]{:S(2)}, u32[]{:S(2)}) collective-permute-start(f32[256,2048]{1,0:T(8,128)S(1)} %add.189), channel_id=1, source_target_pairs={{0,128},{8,136},{16,144},{24,152},{32,160},{40,168},{48,176},{56,1... | collective-permute-start | bytes 6291464 | tf_op jit(solution)/shard_map/ppermute | solution.py:16
  1063.0 62.8 %copy-start.4 = (f32[256,512]{1,0:T(8,128)S(1)}, f32[256,512]{1,0:T(8,128)}, u32[]{:S(2)}) copy-start(f32[256,512]{1,0:T(8,128)} %get-tuple-element.46) | copy-start | bytes 1572868
Sparse Core Ops, SparseCore 0:
  417.1 95.7 all-reduce.15
  987.1 75.8 all-reduce.13
